TPU v7x, 512 devices: a whole 4x8x8 slice. The times are simulated.
512 devices in a mesh: dp: 32 (over x, z), tensor: 16 (over y, core).
Axes of the slice: x: 4, y: 8, z: 8, core: 2. Of those that a mesh axis runs over, the one named last changes fastest.
Arguments:
- tokens: bfloat16 [512, 3072], P('dp'), may hold values from -6 to 6
- cotangent: bfloat16 [512, 3072], P('dp'), may hold values from -6 to 6
- routes: int32 [512, 2], P('dp'), may hold values from 0 to 7, all different within a row; in each aligned block of 16 rows (0 to 15, 16 to 31, ...) at most 8 rows name the same one
- gates: float32 [512, 2], P('dp'), may hold values from 0.2 to 1
- w_gate: bfloat16 [3072, 131072], P(None, ('dp', 'tensor')), may hold values from -0.109375 to 0.109375
- w_up: bfloat16 [3072, 131072], P(None, ('dp', 'tensor')), may hold values from -0.109375 to 0.109375
- w_down: bfloat16 [131072, 3072], P('dp', 'tensor'), may hold values from -0.046875 to 0.046875
Outputs:
- mixed_out: bfloat16 [512, 3072], P('dp', 'tensor')
- d_tokens: bfloat16 [512, 3072], P('dp', 'tensor')
Inputs may be any that keep to these rules, and one draw needn't show every extreme that they name: `routes`: among the tokens of one index of dp (aligned blocks of 16 rows) no expert is chosen more than 8 times, and some expert is chosen exactly 8 times; the 2 experts of a token differ.
All inputs are finite; a program needn't handle non-finite values.
Results may differ from a plain program's by a relative error of at most 0.0057.
Values may be sent and summed in bfloat16 or wider, within the bound.
No kernel may reach another device: no remote copies, remote signals or barrier semaphores. Data moves between devices by JAX's collectives and lax.ppermute only.
A program may use at most 64 MiB of HBM per device.

v0:
```python
import jax
import jax.numpy as jnp
from jax import lax
from jax.sharding import PartitionSpec as P

EXPERTS = 8
CAP = 8


def dot_last(left, right):
    return lax.dot_general(
        left, right, (((1,), (1,)), ((), ())), preferred_element_type=jnp.float32
    )


def body(tokens, cotangent, routes, gates, w_gate, w_up, w_down):
    count_tok, model_width = tokens.shape
    top_k = routes.shape[1]
    n_data = lax.axis_size("dp")
    copies = n_data // EXPERTS
    slot_count = EXPERTS * CAP
    flat_routes = routes.reshape(-1)
    onehot = (flat_routes[:, None] == jnp.arange(EXPERTS, dtype=jnp.int32)[None, :]).astype(
        jnp.int32
    )
    before = jnp.cumsum(onehot, axis=0) - onehot
    target = flat_routes * CAP + jnp.sum(before * onehot, axis=1)
    placing = jnp.arange(slot_count, dtype=jnp.int32)[:, None] == target[None, :]
    place_half = placing.astype(jnp.bfloat16)
    place_full = placing.astype(jnp.float32)
    x_rows = jnp.repeat(tokens, top_k, axis=0)
    dy_rows = (
        jnp.repeat(cotangent.astype(jnp.float32), top_k, axis=0) * gates.reshape(-1)[:, None]
    ).astype(jnp.bfloat16)

    def outbox(rows):
        packed = jnp.dot(place_half, rows, preferred_element_type=jnp.float32).astype(jnp.bfloat16)
        packed = packed.reshape(EXPERTS, CAP, rows.shape[1])
        return jnp.repeat(packed, copies, axis=0)

    got_x, got_dy = (
        lax.all_to_all(outbox(x_rows), "dp", split_axis=0, concat_axis=0, tiled=True),
        lax.all_to_all(outbox(dy_rows), "dp", split_axis=0, concat_axis=0, tiled=True),
    )
    rows_in = got_x.shape[0] * got_x.shape[1]
    x_in = got_x.reshape(rows_in, model_width)
    dy_in = got_dy.reshape(rows_in, model_width)
    gate_pre = jnp.dot(x_in, w_gate, preferred_element_type=jnp.float32)
    up_pre = jnp.dot(x_in, w_up, preferred_element_type=jnp.float32)
    sigmoid_gate = jax.nn.sigmoid(gate_pre)
    activated = gate_pre * sigmoid_gate
    hidden = (activated * up_pre).astype(jnp.bfloat16)
    col_width = w_down.shape[1]
    out_part = jnp.dot(
        lax.all_gather(hidden, "tensor", axis=1, tiled=True),
        w_down,
        preferred_element_type=jnp.float32,
    )
    gate_turned, up_turned, down_turned = (
        lax.all_to_all(w_gate, "tensor", split_axis=0, concat_axis=1, tiled=True),
        lax.all_to_all(w_up, "tensor", split_axis=0, concat_axis=1, tiled=True),
        lax.all_to_all(w_down, "tensor", split_axis=0, concat_axis=1, tiled=True),
    )
    d_hidden = dot_last(dy_in, down_turned)
    d_gate = (d_hidden * up_pre * sigmoid_gate * (1.0 + gate_pre * (1.0 - sigmoid_gate))).astype(
        jnp.bfloat16
    )
    d_up = (d_hidden * activated).astype(jnp.bfloat16)
    grad_part = dot_last(
        lax.all_gather(d_gate, "tensor", axis=1, tiled=True), gate_turned
    ) + dot_last(lax.all_gather(d_up, "tensor", axis=1, tiled=True), up_turned)
    back_out, back_grad = (
        lax.all_to_all(
            out_part.reshape(n_data, CAP, col_width), "dp", split_axis=0, concat_axis=0, tiled=True
        ),
        lax.all_to_all(
            grad_part.reshape(n_data, CAP, col_width), "dp", split_axis=0, concat_axis=0, tiled=True
        ),
    )

    def unpack(returned):
        summed = jnp.sum(returned.reshape(EXPERTS, copies, CAP, col_width), axis=1).reshape(
            slot_count, col_width
        )
        picked = lax.dot_general(
            place_full,
            summed,
            (((0,), (0,)), ((), ())),
            precision=lax.Precision.HIGHEST,
            preferred_element_type=jnp.float32,
        )
        return picked.reshape(count_tok, top_k, col_width)

    mixed_out = jnp.sum(unpack(back_out) * gates[:, :, None], axis=1).astype(jnp.bfloat16)
    d_tokens = jnp.sum(unpack(back_grad), axis=1).astype(jnp.bfloat16)
    return (mixed_out, d_tokens)


def solution(mesh):
    placed = (
        P("dp", None),
        P("dp", None),
        P("dp", None),
        P("dp", None),
        P(None, ("dp", "tensor")),
        P(None, ("dp", "tensor")),
        P("dp", "tensor"),
    )
    return jax.shard_map(
        body,
        mesh=mesh,
        in_specs=placed,
        out_specs=(P("dp", "tensor"), P("dp", "tensor")),
        check_vma=False,
    )
```

profile of v0, /device:TPU:8, one launch (start us, length us, event | category | flops | bytes accessed | tf_op | source)
XLA Modules:
  0.0 352.8 jit_solution(13465686441488400917)
XLA Ops:
  7.2 2.7 copy.46
  9.9 9.5 %all-to-all-start.3 = ((bf16[16,256,192]{1,2,0:T(8,128)(2,1)}), bf16[16,256,192]{1,2,0:T(8,128)(2,1)S(1)}, u32[]{:S(2)}, u32[]{:S(2)}) async-start(bf16[16,256,192]{1,2,0:T(8,128)(2,1)} %bitcast.57), calls=%async_computation.3 | async-start | bytes 3145728 | tf_op jit(solution)/shard_map/all_to_all | solution.py:62
  20.3 35.1 %all-to-all-done.3 = bf16[16,256,192]{1,2,0:T(8,128)(2,1)S(1)} async-done(((bf16[16,256,192]{1,2,0:T(8,128)(2,1)}), bf16[16,256,192]{1,2,0:T(8,128)(2,1)S(1)}, u32[]{:S(2)}, u32[]{:S(2)}) %all-to-all-start.3) | async-done | bytes 1572896 | tf_op jit(solution)/shard_map/all_to_all | solution.py:62
  55.4 1.5 broadcast_in_dim.17
  57.0 11.4 %all-to-all-start = ((bf16[32,8,3072]{2,1,0:T(8,128)(2,1)}), bf16[32,8,3072]{2,1,0:T(8,128)(2,1)S(1)}, u32[]{:S(2)}, u32[]{:S(2)}) async-start(bf16[32,8,3072]{2,1,0:T(8,128)(2,1)} %bitcast.1), calls=%async_computation | async-start | bytes 3145728 | tf_op jit(solution)/shard_map/all_to_all | solution.py:42
  69.4 38.8 %all-to-all-done = bf16[32,8,3072]{2,1,0:T(8,128)(2,1)S(1)} async-done(((bf16[32,8,3072]{2,1,0:T(8,128)(2,1)}), bf16[32,8,3072]{2,1,0:T(8,128)(2,1)S(1)}, u32[]{:S(2)}, u32[]{:S(2)}) %all-to-all-start) | async-done | bytes 1572896 | tf_op jit(solution)/shard_map/all_to_all | solution.py:42
  108.1 1.3 broadcast_in_dim.19
  109.5 5.8 %all-to-all-start.2 = ((bf16[32,8,3072]{2,1,0:T(8,128)(2,1)}), bf16[32,8,3072]{2,1,0:T(8,128)(2,1)}, u32[]{:S(2)}, u32[]{:S(2)}) async-start(bf16[32,8,3072]{2,1,0:T(8,128)(2,1)} %bitcast.8), calls=%async_computation.2 | async-start | bytes 3145728 | tf_op jit(solution)/shard_map/all_to_all | solution.py:43
  115.4 2.1 fusion.6
  118.8 35.8 %all-to-all-done.2 = bf16[32,8,3072]{2,1,0:T(8,128)(2,1)} async-done(((bf16[32,8,3072]{2,1,0:T(8,128)(2,1)}), bf16[32,8,3072]{2,1,0:T(8,128)(2,1)}, u32[]{:S(2)}, u32[]{:S(2)}) %all-to-all-start.2) | async-done | bytes 1572896 | tf_op jit(solution)/shard_map/all_to_all | solution.py:43
  154.6 3.2 multiply_convert_fusion.1
  158.6 7.0 %all-to-all-start.4 = ((bf16[16,192,256]{2,1,0:T(8,128)(2,1)}), bf16[16,192,256]{2,1,0:T(8,128)(2,1)S(1)}, u32[]{:S(2)}, u32[]{:S(2)}) async-start(bf16[16,192,256]{2,1,0:T(8,128)(2,1)} %bitcast.12), calls=%async_computation.4 | async-start | bytes 3145728 | tf_op jit(solution)/shard_map/all_to_all | solution.py:60
  166.3 40.9 %all-to-all-done.4 = bf16[16,192,256]{2,1,0:T(8,128)(2,1)S(1)} async-done(((bf16[16,192,256]{2,1,0:T(8,128)(2,1)}), bf16[16,192,256]{2,1,0:T(8,128)(2,1)S(1)}, u32[]{:S(2)}, u32[]{:S(2)}) %all-to-all-start.4) | async-done | bytes 1572896 | tf_op jit(solution)/shard_map/all_to_all | solution.py:60
  207.2 8.1 %all-to-all-start.5 = ((bf16[16,192,256]{2,1,0:T(8,128)(2,1)}), bf16[16,192,256]{2,1,0:T(8,128)(2,1)S(1)}, u32[]{:S(2)}, u32[]{:S(2)}) async-start(bf16[16,192,256]{2,1,0:T(8,128)(2,1)} %bitcast.60), calls=%async_computation.5 | async-start | bytes 3145728 | tf_op jit(solution)/shard_map/all_to_all | solution.py:61
  215.3 1.3 copy.39
  216.6 36.5 %all-to-all-done.5 = bf16[16,192,256]{2,1,0:T(8,128)(2,1)S(1)} async-done(((bf16[16,192,256]{2,1,0:T(8,128)(2,1)}), bf16[16,192,256]{2,1,0:T(8,128)(2,1)S(1)}, u32[]{:S(2)}, u32[]{:S(2)}) %all-to-all-start.5) | async-done | bytes 1572896 | tf_op jit(solution)/shard_map/all_to_all | solution.py:61
  253.4 3.6 %convolution_bitcast_fusion = f32[32,8,192]{2,1,0:T(8,128)} fusion(bf16[256,4096]{1,0:T(8,128)(2,1)} %all-gather.4.cloned.1.call-done, bf16[4096,192]{0,1:T(8,128)(2,1)} %param.13), kind=kOutput, calls=%fused_computation.11 | convolution fusion | flops 402653184 | bytes 3866624 | tf_op jit(solution)/shard_map/dot_general | solution.py:54
  257.0 6.0 %all-to-all-start.1 = ((f32[32,8,192]{2,1,0:T(8,128)}), f32[32,8,192]{2,1,0:T(8,128)S(1)}, u32[]{:S(2)}, u32[]{:S(2)}) async-start(f32[32,8,192]{2,1,0:T(8,128)} %convolution_bitcast_fusion), calls=%async_computation.1 | async-start | bytes 524288 | tf_op jit(solution)/shard_map/all_to_all | solution.py:73
  263.0 14.1 %all-gather.6.cloned.1.call-done = bf16[256,4096]{1,0:T(8,128)(2,1)} async-done(((bf16[256,256]{1,0:T(8,128)(2,1)}), bf16[256,4096]{1,0:T(8,128)(2,1)}) %all-gather.6.cloned.1.call-update) | async-done | bytes 2097168 | tf_op jit(solution)/shard_map/all_gather | solution.py:70
  277.0 3.1 fusion.18
  280.1 39.1 %all-gather.8.cloned.1.call-done = bf16[256,4096]{1,0:T(8,128)(2,1)} async-done(((bf16[256,256]{1,0:T(8,128)(2,1)}), bf16[256,4096]{1,0:T(8,128)(2,1)}) %all-gather.8.cloned.1.call-update) | async-done | bytes 2097168 | tf_op jit(solution)/shard_map/all_gather | solution.py:71
  319.3 2.4 convolution_add_fusion
  322.5 10.2 %all-to-all-start.6 = ((f32[32,8,192]{2,1,0:T(8,128)}), f32[32,8,192]{2,1,0:T(8,128)S(1)}, u32[]{:S(2)}, u32[]{:S(2)}) async-start(f32[32,8,192]{2,1,0:T(8,128)} %bitcast.16), calls=%async_computation.6 | async-start | bytes 524288 | tf_op jit(solution)/shard_map/all_to_all | solution.py:76
  333.6 11.9 %all-to-all-done.6 = f32[32,8,192]{2,1,0:T(8,128)S(1)} async-done(((f32[32,8,192]{2,1,0:T(8,128)}), f32[32,8,192]{2,1,0:T(8,128)S(1)}, u32[]{:S(2)}, u32[]{:S(2)}) %all-to-all-start.6) | async-done | bytes 196640 | tf_op jit(solution)/shard_map/all_to_all | solution.py:76
  (45 shorter events, 7.4 us)
Async XLA Ops:
  9.9 9.5 %copy-start.3 = (bf16[16,3072]{1,0:T(8,128)(2,1)S(1)}, bf16[16,3072]{1,0:T(8,128)(2,1)}, u32[]{:S(2)}) copy-start(bf16[16,3072]{1,0:T(8,128)(2,1)} %param.7) | copy-start | bytes 294916
  9.9 9.7 %copy-start.6 = (s32[16,2]{0,1:T(2,128)S(1)}, s32[16,2]{0,1:T(2,128)}, u32[]{:S(2)}) copy-start(s32[16,2]{0,1:T(2,128)} %param.9) | copy-start | bytes 388
  9.9 45.5 %all-to-all-start.3 = ((bf16[16,256,192]{1,2,0:T(8,128)(2,1)}), bf16[16,256,192]{1,2,0:T(8,128)(2,1)S(1)}, u32[]{:S(2)}, u32[]{:S(2)}) async-start(bf16[16,256,192]{1,2,0:T(8,128)(2,1)} %bitcast.57), calls=%async_computation.3 | async-start | bytes 3145728 | tf_op jit(solution)/shard_map/all_to_all | solution.py:62
  55.4 1.6 copy-start.2
  56.9 11.6 %copy-start.4 = (bf16[16,3072]{1,0:T(8,128)(2,1)S(1)}, bf16[16,3072]{1,0:T(8,128)(2,1)}, u32[]{:S(2)}) copy-start(bf16[16,3072]{1,0:T(8,128)(2,1)} %param.8) | copy-start | bytes 294916
  56.9 12.0 %copy-start.5 = (f32[16,2]{0,1:T(2,128)S(1)}, f32[16,2]{0,1:T(2,128)}, u32[]{:S(2)}) copy-start(f32[16,2]{0,1:T(2,128)} %param.10) | copy-start | bytes 388
  57.0 51.1 %all-to-all-start = ((bf16[32,8,3072]{2,1,0:T(8,128)(2,1)}), bf16[32,8,3072]{2,1,0:T(8,128)(2,1)S(1)}, u32[]{:S(2)}, u32[]{:S(2)}) async-start(bf16[32,8,3072]{2,1,0:T(8,128)(2,1)} %bitcast.1), calls=%async_computation | async-start | bytes 3145728 | tf_op jit(solution)/shard_map/all_to_all | solution.py:42
  109.5 45.1 %all-to-all-start.2 = ((bf16[32,8,3072]{2,1,0:T(8,128)(2,1)}), bf16[32,8,3072]{2,1,0:T(8,128)(2,1)}, u32[]{:S(2)}, u32[]{:S(2)}) async-start(bf16[32,8,3072]{2,1,0:T(8,128)(2,1)} %bitcast.8), calls=%async_computation.2 | async-start | bytes 3145728 | tf_op jit(solution)/shard_map/all_to_all | solution.py:43
  115.3 2.2 copy-start
  115.3 138.0 %all-gather.4.cloned.1.call-start = ((), (), s32[]{:S(2)}) async-start(), calls=%async_computation.7 | async-start | bytes 2228224 | tf_op jit(solution)/shard_map/all_gather | solution.py:55
  157.8 119.2 %all-gather.6.cloned.1.call-start = ((), (), s32[]{:S(2)}) async-start(), calls=%async_computation.8 | async-start | bytes 2228224 | tf_op jit(solution)/shard_map/all_gather | solution.py:70
  158.6 48.6 %all-to-all-start.4 = ((bf16[16,192,256]{2,1,0:T(8,128)(2,1)}), bf16[16,192,256]{2,1,0:T(8,128)(2,1)S(1)}, u32[]{:S(2)}, u32[]{:S(2)}) async-start(bf16[16,192,256]{2,1,0:T(8,128)(2,1)} %bitcast.12), calls=%async_computation.4 | async-start | bytes 3145728 | tf_op jit(solution)/shard_map/all_to_all | solution.py:60
  165.6 153.7 %all-gather.8.cloned.1.call-start = ((), (), s32[]{:S(2)}) async-start(), calls=%async_computation.9 | async-start | bytes 2228224 | tf_op jit(solution)/shard_map/all_gather | solution.py:71
  207.2 46.0 %all-to-all-start.5 = ((bf16[16,192,256]{2,1,0:T(8,128)(2,1)}), bf16[16,192,256]{2,1,0:T(8,128)(2,1)S(1)}, u32[]{:S(2)}, u32[]{:S(2)}) async-start(bf16[16,192,256]{2,1,0:T(8,128)(2,1)} %bitcast.60), calls=%async_computation.5 | async-start | bytes 3145728 | tf_op jit(solution)/shard_map/all_to_all | solution.py:61
  253.3 23.7 %copy-start.1 = (bf16[16,24,8,256]{3,2,0,1:T(8,128)(2,1)S(1)}, bf16[16,24,8,256]{3,2,0,1:T(8,128)(2,1)}, u32[]{:S(2)}) copy-start(bf16[16,24,8,256]{3,2,0,1:T(8,128)(2,1)} %copy.39) | copy-start | bytes 4718596
  257.0 65.6 %all-to-all-start.1 = ((f32[32,8,192]{2,1,0:T(8,128)}), f32[32,8,192]{2,1,0:T(8,128)S(1)}, u32[]{:S(2)}, u32[]{:S(2)}) async-start(f32[32,8,192]{2,1,0:T(8,128)} %convolution_bitcast_fusion), calls=%async_computation.1 | async-start | bytes 524288 | tf_op jit(solution)/shard_map/all_to_all | solution.py:73
  322.5 23.0 %all-to-all-start.6 = ((f32[32,8,192]{2,1,0:T(8,128)}), f32[32,8,192]{2,1,0:T(8,128)S(1)}, u32[]{:S(2)}, u32[]{:S(2)}) async-start(f32[32,8,192]{2,1,0:T(8,128)} %bitcast.16), calls=%async_computation.6 | async-start | bytes 524288 | tf_op jit(solution)/shard_map/all_to_all | solution.py:76
Sparse Core Ops, SparseCore 0:
  158.0 62.6 all-gather.3
  222.7 54.3 all-gather.5
  279.1 40.1 all-gather.7
where the time goes:
time: 354 us; the launch traced here: 353 us
  waiting for transfers between devices  254 us (72%)
  starting transfers between devices  58.1 us (16%)
  matrix products  17.8 us (5%)
  between operations  13.9 us (4%)
  local copies, waits for them, and re-layouts  8.97 us (3%)
    all_to_all x1, waiting for transfers between devices, body(): lax.all_to_all(w_gate, 'tensor', split_axis=0, concat_axis=1, tiled=True)  40.9 us
    all_gather x1, waiting for transfers between devices, body(): lax.all_gather(d_up, 'tensor', axis=1, tiled=True)  39.1 us
    all_to_all x1, waiting for transfers between devices, body(): lax.all_to_all(outbox(x_rows), 'dp', split_axis=0, concat_axis=0, tiled=T...  38.8 us
    all_to_all x1, waiting for transfers between devices, body(): lax.all_to_all(w_up, 'tensor', split_axis=0, concat_axis=1, tiled=True)  36.5 us
    all_to_all x1, waiting for transfers between devices, body(): lax.all_to_all(outbox(dy_rows), 'dp', split_axis=0, concat_axis=0, tiled=...  35.8 us
    all_to_all x1, waiting for transfers between devices, body(): lax.all_to_all(w_down, 'tensor', split_axis=0, concat_axis=1, tiled=True)  35.1 us
    all_gather x1, waiting for transfers between devices, body(): lax.all_gather(d_gate, 'tensor', axis=1, tiled=True)  14.1 us
    all_to_all x1, waiting for transfers between devices, body(): lax.all_to_all(grad_part.reshape(n_data, CAP, col_width), 'dp', split_axi...  11.9 us
  transfers between devices with their start and end apart: 10, of which 8 were waited for; matrix products, arithmetic and copies ran while one was open for 5% of the time, Pallas kernels for 0%

commit v1 on v0

--- a/solution.py
+++ b/solution.py
@@ -57,7 +57,12 @@
         preferred_element_type=jnp.float32,
     )
     gate_turned, up_turned, down_turned = (
-        lax.all_to_all(w_gate, "tensor", split_axis=0, concat_axis=1, tiled=True),
+        jnp.concatenate(
+            lax.all_to_all(
+                jnp.stack(jnp.split(w_gate, lax.axis_size("tensor"), axis=0)), "tensor", 0, 0
+            ),
+            axis=1,
+        ),
         lax.all_to_all(w_up, "tensor", split_axis=0, concat_axis=1, tiled=True),
         lax.all_to_all(w_down, "tensor", split_axis=0, concat_axis=1, tiled=True),
     )

time: 354 us -> 357 us (level)
  local copies, waits for them, and re-layouts: 8.97 us -> 19.3 us
  waiting for transfers between devices: 254 us -> 249 us
    unnamed x16 -> x33, local copies, waits for them, and re-layouts: 0.36 us -> 10 us
    all_gather x1, waiting for transfers between devices: 14.1 us -> 5.5 us  [body(): lax.all_gather(d_gate, 'tensor', axis=1, tiled=True)]
  transfers between devices with their start and end apart: 10 -> 10, of which waited for: 8 -> 8; matrix products, arithmetic and copies ran while one was open for 5% -> 8% of each run, Pallas kernels for 0% -> 0%
where the time goes in v1:
time: 357 us; the launch traced here: 356 us
  waiting for transfers between devices  249 us (70%)
  starting transfers between devices  56.2 us (16%)
  local copies, waits for them, and re-layouts  19.3 us (5%)
  matrix products  18 us (5%)
  between operations  14 us (4%)
    all_to_all x1, waiting for transfers between devices, body(): lax.all_to_all(jnp.stack(jnp.split(w_gate, lax.axis_size('tensor'), axis=...  41.7 us
    all_gather x1, waiting for transfers between devices, body(): lax.all_gather(d_up, 'tensor', axis=1, tiled=True)  40.2 us
    all_to_all x1, waiting for transfers between devices, body(): lax.all_to_all(w_up, 'tensor', split_axis=0, concat_axis=1, tiled=True)  38.9 us
    all_to_all x1, waiting for transfers between devices, body(): lax.all_to_all(outbox(x_rows), 'dp', split_axis=0, concat_axis=0, tiled=T...  38.8 us
    all_to_all x1, waiting for transfers between devices, body(): lax.all_to_all(outbox(dy_rows), 'dp', split_axis=0, concat_axis=0, tiled=...  35.8 us
    all_to_all x1, waiting for transfers between devices, body(): lax.all_to_all(w_down, 'tensor', split_axis=0, concat_axis=1, tiled=True)  35.1 us
    all_to_all x1, waiting for transfers between devices, body(): lax.all_to_all(grad_part.reshape(n_data, CAP, col_width), 'dp', split_axi...  11.9 us
    all_to_all x1, starting transfers between devices, body(): lax.all_to_all(outbox(x_rows), 'dp', split_axis=0, concat_axis=0, tiled=T...  11.4 us
  transfers between devices with their start and end apart: 10, of which 8 were waited for; matrix products, arithmetic and copies ran while one was open for 8% of the time, Pallas kernels for 0%

profile of v1, /device:TPU:8, one launch (start us, length us, event | category | flops | bytes accessed | tf_op | source)
XLA Modules:
  0.0 356.5 jit_solution(3189994670237564215)
XLA Ops:
  7.2 2.7 copy.46
  9.9 9.5 %all-to-all-start.3 = ((bf16[16,256,192]{1,2,0:T(8,128)(2,1)}), bf16[16,256,192]{1,2,0:T(8,128)(2,1)S(1)}, u32[]{:S(2)}, u32[]{:S(2)}) async-start(bf16[16,256,192]{1,2,0:T(8,128)(2,1)} %bitcast.88), calls=%async_computation.3 | async-start | bytes 3145728 | tf_op jit(solution)/shard_map/all_to_all | solution.py:67
  20.3 35.1 %all-to-all-done.3 = bf16[16,256,192]{1,2,0:T(8,128)(2,1)S(1)} async-done(((bf16[16,256,192]{1,2,0:T(8,128)(2,1)}), bf16[16,256,192]{1,2,0:T(8,128)(2,1)S(1)}, u32[]{:S(2)}, u32[]{:S(2)}) %all-to-all-start.3) | async-done | bytes 1572896 | tf_op jit(solution)/shard_map/all_to_all | solution.py:67
  55.4 1.5 broadcast_in_dim.17
  57.1 11.4 %all-to-all-start = ((bf16[32,8,3072]{2,1,0:T(8,128)(2,1)}), bf16[32,8,3072]{2,1,0:T(8,128)(2,1)S(1)}, u32[]{:S(2)}, u32[]{:S(2)}) async-start(bf16[32,8,3072]{2,1,0:T(8,128)(2,1)} %bitcast.1), calls=%async_computation | async-start | bytes 3145728 | tf_op jit(solution)/shard_map/all_to_all | solution.py:42
  69.4 38.8 %all-to-all-done = bf16[32,8,3072]{2,1,0:T(8,128)(2,1)S(1)} async-done(((bf16[32,8,3072]{2,1,0:T(8,128)(2,1)}), bf16[32,8,3072]{2,1,0:T(8,128)(2,1)S(1)}, u32[]{:S(2)}, u32[]{:S(2)}) %all-to-all-start) | async-done | bytes 1572896 | tf_op jit(solution)/shard_map/all_to_all | solution.py:42
  108.1 1.3 broadcast_in_dim.19
  109.5 5.8 %all-to-all-start.2 = ((bf16[32,8,3072]{2,1,0:T(8,128)(2,1)}), bf16[32,8,3072]{2,1,0:T(8,128)(2,1)}, u32[]{:S(2)}, u32[]{:S(2)}) async-start(bf16[32,8,3072]{2,1,0:T(8,128)(2,1)} %bitcast.8), calls=%async_computation.2 | async-start | bytes 3145728 | tf_op jit(solution)/shard_map/all_to_all | solution.py:43
  115.4 2.1 fusion.6
  118.8 35.8 %all-to-all-done.2 = bf16[32,8,3072]{2,1,0:T(8,128)(2,1)} async-done(((bf16[32,8,3072]{2,1,0:T(8,128)(2,1)}), bf16[32,8,3072]{2,1,0:T(8,128)(2,1)}, u32[]{:S(2)}, u32[]{:S(2)}) %all-to-all-start.2) | async-done | bytes 1572896 | tf_op jit(solution)/shard_map/all_to_all | solution.py:43
  154.6 3.4 multiply_convert_fusion.1
  168.4 6.9 %all-to-all-start.4 = ((bf16[16,192,256]{2,1,0:T(8,128)(2,1)}), bf16[16,192,256]{2,1,0:T(8,128)(2,1)S(1)}, u32[]{:S(2)}, u32[]{:S(2)}) async-start(bf16[16,192,256]{2,1,0:T(8,128)(2,1)} %bitcast_dynamic-update-slice_fusion), calls=%async_computation.4 | async-start | bytes 3145728 | tf_op jit(solution)/shard_map/all_to_all | solution.py:61
  176.1 41.7 %all-to-all-done.4 = bf16[16,192,256]{2,1,0:T(8,128)(2,1)S(1)} async-done(((bf16[16,192,256]{2,1,0:T(8,128)(2,1)}), bf16[16,192,256]{2,1,0:T(8,128)(2,1)S(1)}, u32[]{:S(2)}, u32[]{:S(2)}) %all-to-all-start.4) | async-done | bytes 1572896 | tf_op jit(solution)/shard_map/all_to_all | solution.py:61
  217.7 5.4 %all-to-all-start.5 = ((bf16[16,192,256]{2,1,0:T(8,128)(2,1)}), bf16[16,192,256]{2,1,0:T(8,128)(2,1)S(1)}, u32[]{:S(2)}, u32[]{:S(2)}) async-start(bf16[16,192,256]{2,1,0:T(8,128)(2,1)} %bitcast.91), calls=%async_computation.5 | async-start | bytes 3145728 | tf_op jit(solution)/shard_map/all_to_all | solution.py:66
  223.2 1.3 copy.39
  224.5 38.9 %all-to-all-done.5 = bf16[16,192,256]{2,1,0:T(8,128)(2,1)S(1)} async-done(((bf16[16,192,256]{2,1,0:T(8,128)(2,1)}), bf16[16,192,256]{2,1,0:T(8,128)(2,1)S(1)}, u32[]{:S(2)}, u32[]{:S(2)}) %all-to-all-start.5) | async-done | bytes 1572896 | tf_op jit(solution)/shard_map/all_to_all | solution.py:66
  263.6 3.6 %convolution_bitcast_fusion = f32[32,8,192]{2,1,0:T(8,128)} fusion(bf16[256,4096]{1,0:T(8,128)(2,1)} %all-gather.4.cloned.1.call-done, bf16[4096,192]{0,1:T(8,128)(2,1)} %param.13), kind=kOutput, calls=%fused_computation.11 | convolution fusion | flops 402653184 | bytes 3866624 | tf_op jit(solution)/shard_map/dot_general | solution.py:54
  267.2 6.8 %all-to-all-start.1 = ((f32[32,8,192]{2,1,0:T(8,128)}), f32[32,8,192]{2,1,0:T(8,128)S(1)}, u32[]{:S(2)}, u32[]{:S(2)}) async-start(f32[32,8,192]{2,1,0:T(8,128)} %convolution_bitcast_fusion), calls=%async_computation.1 | async-start | bytes 524288 | tf_op jit(solution)/shard_map/all_to_all | solution.py:78
  274.1 5.5 %all-gather.6.cloned.1.call-done = bf16[256,4096]{1,0:T(8,128)(2,1)} async-done(((bf16[256,256]{1,0:T(8,128)(2,1)}), bf16[256,4096]{1,0:T(8,128)(2,1)}) %all-gather.6.cloned.1.call-update) | async-done | bytes 2097168 | tf_op jit(solution)/shard_map/all_gather | solution.py:75
  279.6 3.1 fusion.18
  282.7 40.2 %all-gather.8.cloned.1.call-done = bf16[256,4096]{1,0:T(8,128)(2,1)} async-done(((bf16[256,256]{1,0:T(8,128)(2,1)}), bf16[256,4096]{1,0:T(8,128)(2,1)}) %all-gather.8.cloned.1.call-update) | async-done | bytes 2097168 | tf_op jit(solution)/shard_map/all_gather | solution.py:76
  322.9 2.4 convolution_add_fusion
  326.2 10.2 %all-to-all-start.6 = ((f32[32,8,192]{2,1,0:T(8,128)}), f32[32,8,192]{2,1,0:T(8,128)S(1)}, u32[]{:S(2)}, u32[]{:S(2)}) async-start(f32[32,8,192]{2,1,0:T(8,128)} %bitcast.31), calls=%async_computation.6 | async-start | bytes 524288 | tf_op jit(solution)/shard_map/all_to_all | solution.py:81
  337.3 11.9 %all-to-all-done.6 = f32[32,8,192]{2,1,0:T(8,128)S(1)} async-done(((f32[32,8,192]{2,1,0:T(8,128)}), f32[32,8,192]{2,1,0:T(8,128)S(1)}, u32[]{:S(2)}, u32[]{:S(2)}) %all-to-all-start.6) | async-done | bytes 196640 | tf_op jit(solution)/shard_map/all_to_all | solution.py:81
  (63 shorter events, 17.1 us)
Async XLA Ops:
  9.9 9.5 %copy-start.4 = (bf16[16,3072]{1,0:T(8,128)(2,1)S(1)}, bf16[16,3072]{1,0:T(8,128)(2,1)}, u32[]{:S(2)}) copy-start(bf16[16,3072]{1,0:T(8,128)(2,1)} %param.7) | copy-start | bytes 294916
  9.9 9.7 %copy-start.7 = (s32[16,2]{0,1:T(2,128)S(1)}, s32[16,2]{0,1:T(2,128)}, u32[]{:S(2)}) copy-start(s32[16,2]{0,1:T(2,128)} %param.9) | copy-start | bytes 388
  9.9 45.5 %all-to-all-start.3 = ((bf16[16,256,192]{1,2,0:T(8,128)(2,1)}), bf16[16,256,192]{1,2,0:T(8,128)(2,1)S(1)}, u32[]{:S(2)}, u32[]{:S(2)}) async-start(bf16[16,256,192]{1,2,0:T(8,128)(2,1)} %bitcast.88), calls=%async_computation.3 | async-start | bytes 3145728 | tf_op jit(solution)/shard_map/all_to_all | solution.py:67
  55.4 1.6 copy-start.3
  56.9 11.6 %copy-start.5 = (bf16[16,3072]{1,0:T(8,128)(2,1)S(1)}, bf16[16,3072]{1,0:T(8,128)(2,1)}, u32[]{:S(2)}) copy-start(bf16[16,3072]{1,0:T(8,128)(2,1)} %param.8) | copy-start | bytes 294916
  56.9 12.0 %copy-start.6 = (f32[16,2]{0,1:T(2,128)S(1)}, f32[16,2]{0,1:T(2,128)}, u32[]{:S(2)}) copy-start(f32[16,2]{0,1:T(2,128)} %param.10) | copy-start | bytes 388
  57.1 51.1 %all-to-all-start = ((bf16[32,8,3072]{2,1,0:T(8,128)(2,1)}), bf16[32,8,3072]{2,1,0:T(8,128)(2,1)S(1)}, u32[]{:S(2)}, u32[]{:S(2)}) async-start(bf16[32,8,3072]{2,1,0:T(8,128)(2,1)} %bitcast.1), calls=%async_computation | async-start | bytes 3145728 | tf_op jit(solution)/shard_map/all_to_all | solution.py:42
  109.5 45.1 %all-to-all-start.2 = ((bf16[32,8,3072]{2,1,0:T(8,128)(2,1)}), bf16[32,8,3072]{2,1,0:T(8,128)(2,1)}, u32[]{:S(2)}, u32[]{:S(2)}) async-start(bf16[32,8,3072]{2,1,0:T(8,128)(2,1)} %bitcast.8), calls=%async_computation.2 | async-start | bytes 3145728 | tf_op jit(solution)/shard_map/all_to_all | solution.py:43
  115.3 2.2 copy-start
  115.3 148.3 %all-gather.4.cloned.1.call-start = ((), (), s32[]{:S(2)}) async-start(), calls=%async_computation.7 | async-start | bytes 2228224 | tf_op jit(solution)/shard_map/all_gather | solution.py:55
  154.6 3.5 copy-start.2
  158.0 121.6 %all-gather.6.cloned.1.call-start = ((), (), s32[]{:S(2)}) async-start(), calls=%async_computation.8 | async-start | bytes 2228224 | tf_op jit(solution)/shard_map/all_gather | solution.py:75
  168.4 49.4 %all-to-all-start.4 = ((bf16[16,192,256]{2,1,0:T(8,128)(2,1)}), bf16[16,192,256]{2,1,0:T(8,128)(2,1)S(1)}, u32[]{:S(2)}, u32[]{:S(2)}) async-start(bf16[16,192,256]{2,1,0:T(8,128)(2,1)} %bitcast_dynamic-update-slice_fusion), calls=%async_computation.4 | async-start | bytes 3145728 | tf_op jit(solution)/shard_map/all_to_all | solution.py:61
  175.3 147.6 %all-gather.8.cloned.1.call-start = ((), (), s32[]{:S(2)}) async-start(), calls=%async_computation.9 | async-start | bytes 2228224 | tf_op jit(solution)/shard_map/all_gather | solution.py:76
  217.7 45.7 %all-to-all-start.5 = ((bf16[16,192,256]{2,1,0:T(8,128)(2,1)}), bf16[16,192,256]{2,1,0:T(8,128)(2,1)S(1)}, u32[]{:S(2)}, u32[]{:S(2)}) async-start(bf16[16,192,256]{2,1,0:T(8,128)(2,1)} %bitcast.91), calls=%async_computation.5 | async-start | bytes 3145728 | tf_op jit(solution)/shard_map/all_to_all | solution.py:66
  263.6 16.0 %copy-start.1 = (bf16[16,24,8,256]{3,2,0,1:T(8,128)(2,1)S(1)}, bf16[16,24,8,256]{3,2,0,1:T(8,128)(2,1)}, u32[]{:S(2)}) copy-start(bf16[16,24,8,256]{3,2,0,1:T(8,128)(2,1)} %copy.39) | copy-start | bytes 4718596
  267.2 59.0 %all-to-all-start.1 = ((f32[32,8,192]{2,1,0:T(8,128)}), f32[32,8,192]{2,1,0:T(8,128)S(1)}, u32[]{:S(2)}, u32[]{:S(2)}) async-start(f32[32,8,192]{2,1,0:T(8,128)} %convolution_bitcast_fusion), calls=%async_computation.1 | async-start | bytes 524288 | tf_op jit(solution)/shard_map/all_to_all | solution.py:78
  326.2 23.0 %all-to-all-start.6 = ((f32[32,8,192]{2,1,0:T(8,128)}), f32[32,8,192]{2,1,0:T(8,128)S(1)}, u32[]{:S(2)}, u32[]{:S(2)}) async-start(f32[32,8,192]{2,1,0:T(8,128)} %bitcast.31), calls=%async_computation.6 | async-start | bytes 524288 | tf_op jit(solution)/shard_map/all_to_all | solution.py:81
Sparse Core Ops, SparseCore 0:
  158.1 64.8 all-gather.3
  225.1 54.4 all-gather.5
  281.6 41.2 all-gather.7
